TPU v7x, 32 devices: a whole 2x2x4 slice. The times are simulated.
32 devices in a mesh: dp: 8 (over z, x), fsdp: 4 (over y, core).
Axes of the slice: x: 2, y: 2, z: 4, core: 2. Of those that a mesh axis runs over, the one named last changes fastest.
Arguments:
- tokens: bfloat16 [8192, 2048], P(('dp', 'fsdp')), may hold values from -6 to 6
- segments: int32 [8192], P(('dp', 'fsdp')), may hold values from 0 to 3, as said below
- gain_attn: float32 [2048], P('dp'), may hold values from 0.1 to 1.9
- w_query: float32 [2048, 2048], P('dp', 'fsdp'), may hold values from -0.125 to 0.125
- w_key: float32 [2048, 256], P('dp', 'fsdp'), may hold values from -0.125 to 0.125
- w_value: float32 [2048, 256], P('dp', 'fsdp'), may hold values from -0.125 to 0.125
- w_out: float32 [2048, 2048], P('fsdp', 'dp'), may hold values from -0.75 to 0.75
- gain_mlp: float32 [2048], P('dp'), may hold values from 0.1 to 1.9
- w_gate: float32 [2048, 5632], P('dp', 'fsdp'), may hold values from -0.125 to 0.125
- w_up: float32 [2048, 5632], P('dp', 'fsdp'), may hold values from -0.125 to 0.125
- w_down: float32 [5632, 2048], P('fsdp', 'dp'), may hold values from -0.078125 to 0.078125
- cotangent: bfloat16 [8192, 2048], P(('dp', 'fsdp')), may hold values from -6 to 6
Outputs:
- layer_out: bfloat16 [8192, 2048], P(('dp', 'fsdp'))
- grad_tokens: bfloat16 [8192, 2048], P(('dp', 'fsdp'))
- grad_gain_attn: float32 [2048], P('dp')
- grad_w_query: float32 [2048, 2048], P('dp', 'fsdp')
- grad_w_key: float32 [2048, 256], P('dp', 'fsdp')
- grad_w_value: float32 [2048, 256], P('dp', 'fsdp')
- grad_w_out: float32 [2048, 2048], P('fsdp', 'dp')
- grad_gain_mlp: float32 [2048], P('dp')
- grad_w_gate: float32 [2048, 5632], P('dp', 'fsdp')
- grad_w_up: float32 [2048, 5632], P('dp', 'fsdp')
- grad_w_down: float32 [5632, 2048], P('fsdp', 'dp')
Inputs may be any that keep to these rules, and one draw needn't show every extreme that they name: `segments`: on each device's 256 tokens the ids number 1 to 4 whole sequences from 0 up, never falling; every sequence has 64, 128 or 256 tokens; some device holds one sequence and some four.
All inputs are finite; a program needn't handle non-finite values.
Results may differ from a plain program's by a relative error of at most 0.02.
Values may be sent and summed in bfloat16 or wider, within the bound.
No kernel may reach another device: no remote copies, remote signals or barrier semaphores. Data moves between devices by JAX's collectives and lax.ppermute only.
A program may use at most 448 MiB of HBM per device.

v0:
```python
import math
import jax
import jax.numpy as jnp
from jax import lax
from jax.sharding import PartitionSpec as P

HEAD_DIM = 64
EPSILON = 1e-05
rope_base = 10000.0


def tables(segment_block):
    rows_here = segment_block.shape[0]
    places = jnp.arange(rows_here, dtype=jnp.int32)
    same_segment = segment_block[:, None] == segment_block[None, :]
    first_index = jnp.min(jnp.where(same_segment, places[None, :], rows_here), axis=1)
    offsets = (places - first_index).astype(jnp.float32)
    half_dim = HEAD_DIM // 2
    frequencies = jnp.exp(
        jnp.arange(half_dim, dtype=jnp.float32) * (-2.0 * math.log(rope_base) / HEAD_DIM)
    )
    angles = offsets[:, None] * frequencies[None, :]
    cosine = jnp.concatenate([jnp.cos(angles), jnp.cos(angles)], axis=1)[:, None, :]
    sine_part = jnp.concatenate([jnp.sin(angles), jnp.sin(angles)], axis=1)[:, None, :]
    allowed = same_segment & (places[:, None] >= places[None, :])
    return (cosine, sine_part, allowed)


def rotate(values, cosine, sine_part):
    half_dim = values.shape[-1] // 2
    turned = jnp.concatenate([-values[..., half_dim:], values[..., :half_dim]], axis=-1)
    return values * cosine + turned * sine_part


def group_inputs(tokens, segments, cotangent):
    return (tokens, segments, cotangent, 1)


def attention_weights(gain_attn, w_query, w_key, w_value, w_out):
    low_type = jnp.bfloat16
    rows_full = (
        lax.all_gather(gain_attn.astype(low_type), "dp", axis=0, tiled=True),
        lax.all_gather(w_query.astype(low_type), "dp", axis=0, tiled=True),
        lax.all_gather(w_key.astype(low_type), "dp", axis=0, tiled=True),
        lax.all_gather(w_value.astype(low_type), "dp", axis=0, tiled=True),
        lax.all_gather(w_out.astype(low_type), "dp", axis=1, tiled=True),
    )
    wide_cols = (
        lax.all_gather(rows_full[1], "fsdp", axis=1, tiled=True),
        lax.all_gather(rows_full[2], "fsdp", axis=1, tiled=True),
        lax.all_gather(rows_full[3], "fsdp", axis=1, tiled=True),
        lax.all_gather(rows_full[4], "fsdp", axis=0, tiled=True),
    )
    return (rows_full[0], wide_cols[0], wide_cols[1], wide_cols[2], wide_cols[3])


def feed_weights(gain_mlp, w_gate, w_up, w_down):
    low_type = jnp.bfloat16
    rows_full = (
        lax.all_gather(gain_mlp.astype(low_type), "dp", axis=0, tiled=True),
        lax.all_gather(w_gate.astype(low_type), "dp", axis=0, tiled=True),
        lax.all_gather(w_up.astype(low_type), "dp", axis=0, tiled=True),
        lax.all_gather(w_down.astype(low_type), "dp", axis=1, tiled=True),
    )
    wide_cols = (
        lax.all_gather(rows_full[1], "fsdp", axis=1, tiled=True),
        lax.all_gather(rows_full[2], "fsdp", axis=1, tiled=True),
        lax.all_gather(rows_full[3], "fsdp", axis=0, tiled=True),
    )
    return (rows_full[0], wide_cols[0], wide_cols[1], wide_cols[2])


def reduce_attention(grad_gain, grad_query, grad_key, grad_value, grad_output):
    terms = (
        lax.psum_scatter(
            jnp.tile(grad_gain, lax.axis_size("fsdp")).astype(jnp.bfloat16),
            "fsdp",
            scatter_dimension=0,
            tiled=True,
        ).astype(jnp.float32),
        lax.psum_scatter(
            grad_query.astype(jnp.bfloat16), "fsdp", scatter_dimension=1, tiled=True
        ).astype(jnp.float32),
        lax.psum_scatter(
            grad_key.astype(jnp.bfloat16), "fsdp", scatter_dimension=1, tiled=True
        ).astype(jnp.float32),
        lax.psum_scatter(
            grad_value.astype(jnp.bfloat16), "fsdp", scatter_dimension=1, tiled=True
        ).astype(jnp.float32),
        lax.psum_scatter(
            grad_output.astype(jnp.bfloat16), "fsdp", scatter_dimension=0, tiled=True
        ).astype(jnp.float32),
    )
    return (
        lax.psum_scatter(
            terms[0].astype(jnp.bfloat16), "dp", scatter_dimension=0, tiled=True
        ).astype(jnp.float32),
        lax.psum_scatter(
            terms[1].astype(jnp.bfloat16), "dp", scatter_dimension=0, tiled=True
        ).astype(jnp.float32),
        lax.psum_scatter(
            terms[2].astype(jnp.bfloat16), "dp", scatter_dimension=0, tiled=True
        ).astype(jnp.float32),
        lax.psum_scatter(
            terms[3].astype(jnp.bfloat16), "dp", scatter_dimension=0, tiled=True
        ).astype(jnp.float32),
        lax.psum_scatter(
            terms[4].astype(jnp.bfloat16), "dp", scatter_dimension=1, tiled=True
        ).astype(jnp.float32),
    )


def reduce_feed(grad_gain, grad_gate, grad_upward, grad_down):
    terms = (
        lax.psum_scatter(
            jnp.tile(grad_gain, lax.axis_size("fsdp")).astype(jnp.bfloat16),
            "fsdp",
            scatter_dimension=0,
            tiled=True,
        ).astype(jnp.float32),
        lax.psum_scatter(
            grad_gate.astype(jnp.bfloat16), "fsdp", scatter_dimension=1, tiled=True
        ).astype(jnp.float32),
        lax.psum_scatter(
            grad_upward.astype(jnp.bfloat16), "fsdp", scatter_dimension=1, tiled=True
        ).astype(jnp.float32),
        lax.psum_scatter(
            grad_down.astype(jnp.bfloat16), "fsdp", scatter_dimension=0, tiled=True
        ).astype(jnp.float32),
    )
    return (
        lax.psum_scatter(
            terms[0].astype(jnp.bfloat16), "dp", scatter_dimension=0, tiled=True
        ).astype(jnp.float32),
        lax.psum_scatter(
            terms[1].astype(jnp.bfloat16), "dp", scatter_dimension=0, tiled=True
        ).astype(jnp.float32),
        lax.psum_scatter(
            terms[2].astype(jnp.bfloat16), "dp", scatter_dimension=0, tiled=True
        ).astype(jnp.float32),
        lax.psum_scatter(
            terms[3].astype(jnp.bfloat16), "dp", scatter_dimension=1, tiled=True
        ).astype(jnp.float32),
    )


def on_device(
    tokens,
    segments,
    gain_attn,
    w_query,
    w_key,
    w_value,
    w_out,
    gain_mlp,
    w_gate,
    w_up,
    w_down,
    cotangent,
):
    low_type = jnp.bfloat16
    wide_type = jnp.float32
    score_scale = HEAD_DIM ** (-0.5)
    token_rows, segment_rows, cotangent_rows, blocks = group_inputs(tokens, segments, cotangent)
    rows_all = token_rows.shape[0]
    block_rows = rows_all // blocks
    attn_full = attention_weights(gain_attn, w_query, w_key, w_value, w_out)
    feed_full = feed_weights(gain_mlp, w_gate, w_up, w_down)
    gain_one = attn_full[0].astype(wide_type)
    query_full, key_full, value_full, out_full = (
        attn_full[1],
        attn_full[2],
        attn_full[3],
        attn_full[4],
    )
    gain_two = feed_full[0].astype(wide_type)
    gate_full, up_full, down_full = (feed_full[1], feed_full[2], feed_full[3])
    heads_here = query_full.shape[1] // HEAD_DIM
    kv_here = key_full.shape[1] // HEAD_DIM
    group_size = heads_here // kv_here
    token_float = token_rows.astype(wide_type)
    inv_first = lax.rsqrt(jnp.mean(token_float * token_float, axis=-1, keepdims=True) + EPSILON)
    unit_attn = token_float * inv_first
    normed = (unit_attn * gain_one).astype(low_type)
    cosine, sine_part, allowed = jax.vmap(tables)(segment_rows.reshape(blocks, block_rows))
    query_proj = jnp.dot(normed, query_full, preferred_element_type=wide_type).reshape(
        blocks, block_rows, heads_here, HEAD_DIM
    )
    keys_proj = jnp.dot(normed, key_full, preferred_element_type=wide_type).reshape(
        blocks, block_rows, kv_here, HEAD_DIM
    )
    values_low = (
        jnp.dot(normed, value_full, preferred_element_type=wide_type)
        .astype(low_type)
        .reshape(blocks, block_rows, kv_here, HEAD_DIM)
    )
    query_rot = (
        rotate(query_proj, cosine, sine_part)
        .astype(low_type)
        .reshape(blocks, block_rows, kv_here, group_size, HEAD_DIM)
    )
    keys_rot = rotate(keys_proj, cosine, sine_part).astype(low_type)
    scores = (
        jnp.einsum("btgrd,bugd->bgrtu", query_rot, keys_rot, preferred_element_type=wide_type)
        * score_scale
    )
    masked = jnp.where(allowed[:, None, None], scores, -1e30)
    row_peak = jnp.max(masked, axis=-1, keepdims=True)
    exponent = jnp.exp(masked - row_peak)
    row_total = jnp.sum(exponent, axis=-1, keepdims=True)
    weights_soft = exponent / row_total
    log_total = row_peak + jnp.log(row_total)
    mixed_heads = jnp.einsum(
        "bgrtu,bugd->btgrd",
        weights_soft.astype(low_type),
        values_low,
        preferred_element_type=wide_type,
    )
    mixed_heads = mixed_heads.reshape(rows_all, heads_here * HEAD_DIM).astype(low_type)
    hidden = token_float + jnp.dot(mixed_heads, out_full, preferred_element_type=wide_type)
    inv_second = lax.rsqrt(jnp.mean(hidden * hidden, axis=-1, keepdims=True) + EPSILON)
    unit_mlp = hidden * inv_second
    normed_mlp = (unit_mlp * gain_two).astype(low_type)
    gate_proj = jnp.dot(normed_mlp, gate_full, preferred_element_type=wide_type)
    upward = jnp.dot(normed_mlp, up_full, preferred_element_type=wide_type)
    gate_sigmoid = jax.nn.sigmoid(gate_proj)
    activation = (gate_proj * gate_sigmoid * upward).astype(low_type)
    down_terms = jnp.dot(activation, down_full, preferred_element_type=wide_type)
    layer_out = (hidden + down_terms).astype(low_type)
    feed_back = feed_weights(gain_mlp, w_gate, w_up, w_down)
    gate_back, up_back, down_back = (feed_back[1], feed_back[2], feed_back[3])
    grad_down = jnp.einsum(
        "tf,td->fd", activation, cotangent_rows, preferred_element_type=wide_type
    )
    grad_act = jnp.einsum("td,fd->tf", cotangent_rows, down_back, preferred_element_type=wide_type)
    grad_gate = (
        grad_act * upward * gate_sigmoid * (1.0 + gate_proj * (1.0 - gate_sigmoid))
    ).astype(low_type)
    grad_upward = (grad_act * gate_proj * gate_sigmoid).astype(low_type)
    grad_w_gate = jnp.einsum("tc,tf->cf", normed_mlp, grad_gate, preferred_element_type=wide_type)
    grad_w_up = jnp.einsum("tc,tf->cf", normed_mlp, grad_upward, preferred_element_type=wide_type)
    grad_normed_mlp = jnp.einsum(
        "tf,cf->tc", grad_gate, gate_back, preferred_element_type=wide_type
    )
    grad_normed_mlp = grad_normed_mlp + jnp.einsum(
        "tf,cf->tc", grad_upward, up_back, preferred_element_type=wide_type
    )
    grad_gain_mlp = jnp.sum(grad_normed_mlp * unit_mlp, axis=0)
    scaled_mlp = grad_normed_mlp * gain_two
    grad_hidden = cotangent_rows.astype(wide_type) + inv_second * (
        scaled_mlp - unit_mlp * jnp.mean(scaled_mlp * unit_mlp, axis=-1, keepdims=True)
    )
    feed_grads = reduce_feed(grad_gain_mlp, grad_w_gate, grad_w_up, grad_down)
    attn_back = attention_weights(gain_attn, w_query, w_key, w_value, w_out)
    query_back, key_back, value_back, out_back = (
        attn_back[1],
        attn_back[2],
        attn_back[3],
        attn_back[4],
    )
    grad_branch = grad_hidden.astype(low_type)
    grad_w_out = jnp.einsum("tc,td->cd", mixed_heads, grad_branch, preferred_element_type=wide_type)
    grad_mixed = jnp.einsum(
        "td,cd->tc", grad_branch, out_back, preferred_element_type=wide_type
    ).astype(low_type)
    grad_mixed = grad_mixed.reshape(blocks, block_rows, kv_here, group_size, HEAD_DIM)
    scores_again = (
        jnp.einsum("btgrd,bugd->bgrtu", query_rot, keys_rot, preferred_element_type=wide_type)
        * score_scale
    )
    weights_again = jnp.exp(jnp.where(allowed[:, None, None], scores_again, -1e30) - log_total)
    grad_weights = jnp.einsum(
        "btgrd,bugd->bgrtu", grad_mixed, values_low, preferred_element_type=wide_type
    )
    grad_values = jnp.einsum(
        "bgrtu,btgrd->bugd",
        weights_again.astype(low_type),
        grad_mixed,
        preferred_element_type=wide_type,
    )
    grad_values = grad_values.astype(low_type).reshape(rows_all, kv_here * HEAD_DIM)
    row_delta = jnp.sum(weights_again * grad_weights, axis=-1, keepdims=True)
    grad_scores = (weights_again * (grad_weights - row_delta)).astype(low_type)
    grad_query_rot = (
        jnp.einsum("bgrtu,bugd->btgrd", grad_scores, keys_rot, preferred_element_type=wide_type)
        * score_scale
    )
    grad_keys_rot = (
        jnp.einsum("bgrtu,btgrd->bugd", grad_scores, query_rot, preferred_element_type=wide_type)
        * score_scale
    )
    grad_query = (
        rotate(grad_query_rot.reshape(blocks, block_rows, heads_here, HEAD_DIM), cosine, -sine_part)
        .astype(low_type)
        .reshape(rows_all, heads_here * HEAD_DIM)
    )
    grad_keys = (
        rotate(grad_keys_rot, cosine, -sine_part)
        .astype(low_type)
        .reshape(rows_all, kv_here * HEAD_DIM)
    )
    grad_w_query = jnp.einsum("tc,te->ce", normed, grad_query, preferred_element_type=wide_type)
    grad_w_key = jnp.einsum("tc,te->ce", normed, grad_keys, preferred_element_type=wide_type)
    grad_w_value = jnp.einsum("tc,te->ce", normed, grad_values, preferred_element_type=wide_type)
    grad_normed = jnp.einsum("te,ce->tc", grad_query, query_back, preferred_element_type=wide_type)
    grad_normed = grad_normed + jnp.einsum(
        "te,ce->tc", grad_keys, key_back, preferred_element_type=wide_type
    )
    grad_normed = grad_normed + jnp.einsum(
        "te,ce->tc", grad_values, value_back, preferred_element_type=wide_type
    )
    grad_gain_attn = jnp.sum(grad_normed * unit_attn, axis=0)
    scaled_attn = grad_normed * gain_one
    grad_inputs = grad_hidden + inv_first * (
        scaled_attn - unit_attn * jnp.mean(scaled_attn * unit_attn, axis=-1, keepdims=True)
    )
    grad_tokens = grad_inputs.astype(low_type)
    attn_grads = reduce_attention(
        grad_gain_attn, grad_w_query, grad_w_key, grad_w_value, grad_w_out
    )
    return (
        layer_out,
        grad_tokens,
        attn_grads[0],
        attn_grads[1],
        attn_grads[2],
        attn_grads[3],
        attn_grads[4],
        feed_grads[0],
        feed_grads[1],
        feed_grads[2],
        feed_grads[3],
    )


def solution(mesh):
    placed = (
        P(("dp", "fsdp"), None),
        P(("dp", "fsdp")),
        P("dp"),
        P("dp", "fsdp"),
        P("dp", "fsdp"),
        P("dp", "fsdp"),
        P("fsdp", "dp"),
        P("dp"),
        P("dp", "fsdp"),
        P("dp", "fsdp"),
        P("fsdp", "dp"),
        P(("dp", "fsdp"), None),
    )
    return jax.shard_map(
        on_device,
        mesh=mesh,
        in_specs=placed,
        out_specs=(
            P(("dp", "fsdp"), None),
            P(("dp", "fsdp"), None),
            P("dp"),
            P("dp", "fsdp"),
            P("dp", "fsdp"),
            P("dp", "fsdp"),
            P("fsdp", "dp"),
            P("dp"),
            P("dp", "fsdp"),
            P("dp", "fsdp"),
            P("fsdp", "dp"),
        ),
        check_vma=False,
    )
```

profile of v0, /device:TPU:0, one launch (start us, length us, event | category | flops | bytes accessed | tf_op | source)
XLA Modules:
  0.0 2389.2 jit_solution(8841014630282834477)
XLA Ops:
  14.7 35.2 %all_gather.65 = bf16[2048,64]{0,1:T(8,128)(2,1)} all-gather(bf16[256,64]{0,1:T(8,128)(2,1)S(1)} %convert_element_type.225), channel_id=1, replica_groups=mesh['dp'=8,'fsdp'=4] {'dp'}, dimensions={0}, use_global_device_ids=true | all-gather | bytes 294912 | tf_op jit(solution)/shard_map/all_gather | solution.py:44
  50.0 33.1 %all_gather.63 = bf16[2048,64]{0,1:T(8,128)(2,1)} all-gather(bf16[256,64]{0,1:T(8,128)(2,1)S(1)} %convert_element_type.223), channel_id=1, replica_groups=mesh['dp'=8,'fsdp'=4] {'dp'}, dimensions={0}, use_global_device_ids=true | all-gather | bytes 294912 | tf_op jit(solution)/shard_map/all_gather | solution.py:45
  84.0 34.4 %all-gather.23.cloned.1.call-done = bf16[512,2048]{1,0:T(8,128)(2,1)} async-done(((bf16[512,256]{1,0:T(8,128)(2,1)}), bf16[512,2048]{1,0:T(8,128)(2,1)}) %all-gather.23.cloned.1.call-update) | async-done | bytes 2097168 | tf_op jit(solution)/shard_map/all_gather | solution.py:46
  118.4 93.6 %all-gather.27.cloned.1.call-done = bf16[2048,1408]{1,0:T(8,128)(2,1)} async-done(((bf16[256,1408]{1,0:T(8,128)(2,1)}), bf16[2048,1408]{1,0:T(8,128)(2,1)}) %all-gather.27.cloned.1.call-update) | async-done | bytes 5767184 | tf_op jit(solution)/shard_map/all_gather | solution.py:61
  212.1 93.4 %all-gather.31.cloned.1.call-done = bf16[2048,1408]{1,0:T(8,128)(2,1)} async-done(((bf16[256,1408]{1,0:T(8,128)(2,1)}), bf16[2048,1408]{1,0:T(8,128)(2,1)}) %all-gather.31.cloned.1.call-update) | async-done | bytes 5767184 | tf_op jit(solution)/shard_map/all_gather | solution.py:62
  305.5 94.2 %all-gather.35.cloned.1.call-done = bf16[1408,2048]{1,0:T(8,128)(2,1)} async-done(((bf16[1408,256]{1,0:T(8,128)(2,1)}), bf16[1408,2048]{1,0:T(8,128)(2,1)}) %all-gather.35.cloned.1.call-update) | async-done | bytes 5767184 | tf_op jit(solution)/shard_map/all_gather | solution.py:63
  400.4 17.7 all-gather
  418.2 16.8 all-gather.1
  440.3 54.0 %all-gather.21.cloned.1.call-done = bf16[2048,2048]{1,0:T(8,128)(2,1)} async-done(((bf16[2048,512]{1,0:T(8,128)(2,1)}), bf16[2048,2048]{1,0:T(8,128)(2,1)}) %all-gather.21.cloned.1.call-update) | async-done | bytes 8388624 | tf_op jit(solution)/shard_map/all_gather | solution.py:49
  494.3 6.8 fusion.51
  510.3 43.9 %all-gather.25.cloned.1.call-done = bf16[2048,2048]{1,0:T(8,128)(2,1)} async-done(((bf16[512,2048]{1,0:T(8,128)(2,1)}), bf16[2048,2048]{1,0:T(8,128)(2,1)}) %all-gather.25.cloned.1.call-update) | async-done | bytes 8388624 | tf_op jit(solution)/shard_map/all_gather | solution.py:52
  554.2 6.2 multiply_reduce_fusion.2
  562.0 136.7 %all-gather.29.cloned.1.call-done = bf16[2048,5632]{1,0:T(8,128)(2,1)} async-done(((bf16[2048,1408]{1,0:T(8,128)(2,1)}), bf16[2048,5632]{1,0:T(8,128)(2,1)}) %all-gather.29.cloned.1.call-update) | async-done | bytes 23068688 | tf_op jit(solution)/shard_map/all_gather | solution.py:66
  698.8 13.0 fusion.57
  711.8 131.7 %all-gather.33.cloned.1.call-done = bf16[2048,5632]{1,0:T(8,128)(2,1)} async-done(((bf16[2048,1408]{1,0:T(8,128)(2,1)}), bf16[2048,5632]{1,0:T(8,128)(2,1)}) %all-gather.33.cloned.1.call-update) | async-done | bytes 23068688 | tf_op jit(solution)/shard_map/all_gather | solution.py:67
  843.5 13.1 fusion.58
  856.6 131.6 %all-gather.37.cloned.1.call-done = bf16[5632,2048]{1,0:T(8,128)(2,1)} async-done(((bf16[1408,2048]{1,0:T(8,128)(2,1)}), bf16[5632,2048]{1,0:T(8,128)(2,1)}) %all-gather.37.cloned.1.call-update) | async-done | bytes 23068688 | tf_op jit(solution)/shard_map/all_gather | solution.py:68
  988.2 18.6 multiply_convert_fusion
  1006.8 12.6 fusion.59
  1019.4 13.7 multiply_reduce_fusion
  1036.2 6.7 convolution_convert_fusion.7
  1045.1 5.6 fusion
  1057.8 5.1 fusion.35
  1064.7 3.2 convolution_multiply_fusion
  1070.3 5.8 convolution_convert_fusion.4
  1076.2 6.8 convolution_convert_fusion.3
  1083.0 13.0 convolution_convert_fusion.2
  1096.1 30.9 %copy.62 = bf16[2048,5632]{0,1:T(8,128)(2,1)} copy(bf16[2048,5632]{1,0:T(8,128)(2,1)} %convolution_convert_fusion.2) | data formatting | bytes 46137344
  1127.3 13.2 convolution_convert_fusion.1
  1140.5 29.0 %copy.64 = bf16[2048,5632]{0,1:T(8,128)(2,1)} copy(bf16[2048,5632]{1,0:T(8,128)(2,1)} %convolution_convert_fusion.1) | data formatting | bytes 46137344
  1169.5 12.6 convolution_convert_fusion
  1185.1 74.3 %reduce-scatter.31.cloned.1.call-done = bf16[512,2048]{1,0:T(8,128)(2,1)} async-done(((bf16[2048,2048]{1,0:T(8,128)(2,1)}), bf16[512,2048]{1,0:T(8,128)(2,1)}) %reduce-scatter.31.cloned.1.call-update) | async-done | bytes 2097168 | tf_op jit(solution)/shard_map/reduce_scatter | solution.py:90
  1259.4 169.2 %reduce-scatter.43.cloned.1.call-done = bf16[1408,2048]{1,0:T(8,128)(2,1)} async-done(((bf16[5632,2048]{1,0:T(8,128)(2,1)}), bf16[1408,2048]{1,0:T(8,128)(2,1)}) %reduce-scatter.43.cloned.1.call-update) | async-done | bytes 5767184
  1428.6 8.2 copy.63
  1436.9 161.1 %reduce-scatter.45.cloned.1.call-done = bf16[1408,2048]{1,0:T(8,128)(2,1)} async-done(((bf16[5632,2048]{1,0:T(8,128)(2,1)}), bf16[1408,2048]{1,0:T(8,128)(2,1)}) %reduce-scatter.45.cloned.1.call-update) | async-done | bytes 5767184
  1598.0 8.4 copy.65
  1606.5 160.9 %reduce-scatter.39.cloned.1.call-done = bf16[1408,2048]{1,0:T(8,128)(2,1)} async-done(((bf16[5632,2048]{1,0:T(8,128)(2,1)}), bf16[1408,2048]{1,0:T(8,128)(2,1)}) %reduce-scatter.39.cloned.1.call-update) | async-done | bytes 5767184 | tf_op jit(solution)/shard_map/reduce_scatter | solution.py:127
  1770.6 6.2 fusion.60
  1780.2 10.7 all-reduce.5
  1791.0 21.9 all-reduce.4
  1814.2 3.3 fusion.22
  1817.5 12.2 fusion.16
  1834.0 63.0 %reduce-scatter.29.cloned.1.call-done = bf16[256,64]{0,1:T(8,128)(2,1)} async-done(((bf16[2048,64]{0,1:T(8,128)(2,1)}), bf16[256,64]{0,1:T(8,128)(2,1)}) %reduce-scatter.29.cloned.1.call-update) | async-done | bytes 32784 | tf_op jit(solution)/shard_map/reduce_scatter | solution.py:104
  1898.4 69.3 %reduce-scatter.21.cloned.1.call-done = bf16[256,512]{1,0:T(8,128)(2,1)} async-done(((bf16[2048,512]{1,0:T(8,128)(2,1)}), bf16[256,512]{1,0:T(8,128)(2,1)}) %reduce-scatter.21.cloned.1.call-update) | async-done | bytes 262160 | tf_op jit(solution)/shard_map/reduce_scatter | solution.py:98
  1969.5 69.5 %reduce-scatter.33.cloned.1.call-done = bf16[512,256]{1,0:T(8,128)(2,1)} async-done(((bf16[512,2048]{1,0:T(8,128)(2,1)}), bf16[512,256]{1,0:T(8,128)(2,1)}) %reduce-scatter.33.cloned.1.call-update) | async-done | bytes 262160 | tf_op jit(solution)/shard_map/reduce_scatter | solution.py:107
  2040.8 111.1 %reduce-scatter.35.cloned.1.call-done = bf16[256,1408]{1,0:T(8,128)(2,1)} async-done(((bf16[2048,1408]{1,0:T(8,128)(2,1)}), bf16[256,1408]{1,0:T(8,128)(2,1)}) %reduce-scatter.35.cloned.1.call-update) | async-done | bytes 720912 | tf_op jit(solution)/shard_map/reduce_scatter | solution.py:135
  2154.2 111.6 %reduce-scatter.37.cloned.1.call-done = bf16[256,1408]{1,0:T(8,128)(2,1)} async-done(((bf16[2048,1408]{1,0:T(8,128)(2,1)}), bf16[256,1408]{1,0:T(8,128)(2,1)}) %reduce-scatter.37.cloned.1.call-update) | async-done | bytes 720912 | tf_op jit(solution)/shard_map/reduce_scatter | solution.py:138
  2268.1 111.9 %reduce-scatter.41.cloned.1.call-done = bf16[1408,256]{1,0:T(8,128)(2,1)} async-done(((bf16[1408,2048]{1,0:T(8,128)(2,1)}), bf16[1408,256]{1,0:T(8,128)(2,1)}) %reduce-scatter.41.cloned.1.call-update) | async-done | bytes 720912 | tf_op jit(solution)/shard_map/reduce_scatter | solution.py:141
  (185 shorter events, 67.7 us)
Async XLA Ops:
  7.2 3.9 copy-start.9
  7.2 5.0 copy-start.10
  7.2 76.0 %all-gather.19.cloned.1.call-start = ((), (), s32[]{:S(2)}) async-start(), calls=%async_computation.16 | async-start | bytes 2359296 | tf_op jit(solution)/shard_map/all_gather | solution.py:43
  9.2 109.2 %all-gather.23.cloned.1.call-start = ((), (), s32[]{:S(2)}) async-start(), calls=%async_computation.18 | async-start | bytes 2359296 | tf_op jit(solution)/shard_map/all_gather | solution.py:46
  11.0 200.9 %all-gather.27.cloned.1.call-start = ((), (), s32[]{:S(2)}) async-start(), calls=%async_computation.20 | async-start | bytes 6488064 | tf_op jit(solution)/shard_map/all_gather | solution.py:61
  12.0 1.6 copy-start.11
  12.1 2.6 copy-start.20
  12.1 37.9 %copy-start.21 = (f32[256,64]{0,1:T(8,128)S(1)}, f32[256,64]{0,1:T(8,128)}, u32[]{:S(2)}) copy-start(f32[256,64]{0,1:T(8,128)} %param.17) | copy-start | bytes 196612
  12.1 293.4 %all-gather.31.cloned.1.call-start = ((), (), s32[]{:S(2)}) async-start(), calls=%async_computation.22 | async-start | bytes 6488064 | tf_op jit(solution)/shard_map/all_gather | solution.py:62
  13.1 386.6 %all-gather.35.cloned.1.call-start = ((), (), s32[]{:S(2)}) async-start(), calls=%async_computation.24 | async-start | bytes 6488064 | tf_op jit(solution)/shard_map/all_gather | solution.py:63
  14.6 422.0 %all-gather.17.cloned.1.call-start = ((), (), s32[]{:S(2)}) async-start(), calls=%async_computation.15 | async-start | bytes 1310720 | tf_op jit(solution)/shard_map/all_gather | solution.py:50
  49.9 388.5 %all-gather.15.cloned.1.call-start = ((), (), s32[]{:S(2)}) async-start(), calls=%async_computation.14 | async-start | bytes 1310720 | tf_op jit(solution)/shard_map/all_gather | solution.py:51
  83.2 411.2 %all-gather.21.cloned.1.call-start = ((), (), s32[]{:S(2)}) async-start(), calls=%async_computation.17 | async-start | bytes 10485760 | tf_op jit(solution)/shard_map/all_gather | solution.py:49
  83.9 470.3 %all-gather.25.cloned.1.call-start = ((), (), s32[]{:S(2)}) async-start(), calls=%async_computation.19 | async-start | bytes 10485760 | tf_op jit(solution)/shard_map/all_gather | solution.py:52
  118.4 580.4 %all-gather.29.cloned.1.call-start = ((), (), s32[]{:S(2)}) async-start(), calls=%async_computation.21 | async-start | bytes 28835840 | tf_op jit(solution)/shard_map/all_gather | solution.py:66
  212.0 631.5 %all-gather.33.cloned.1.call-start = ((), (), s32[]{:S(2)}) async-start(), calls=%async_computation.23 | async-start | bytes 28835840 | tf_op jit(solution)/shard_map/all_gather | solution.py:67
  305.5 682.7 %all-gather.37.cloned.1.call-start = ((), (), s32[]{:S(2)}) async-start(), calls=%async_computation.25 | async-start | bytes 28835840 | tf_op jit(solution)/shard_map/all_gather | solution.py:68
  399.7 18.4 copy-start.24
  399.7 35.3 %copy-start.22 = (s32[256]{0:T(256)S(1)}, s32[256]{0:T(256)}, u32[]{:S(2)}) copy-start(s32[256]{0:T(256)} %param.13) | copy-start | bytes 3076
  399.7 36.4 %copy-start.2 = (bf16[256,2048]{1,0:T(8,128)(2,1)S(1)}, bf16[256,2048]{1,0:T(8,128)(2,1)}, u32[]{:S(2)}) copy-start(bf16[256,2048]{1,0:T(8,128)(2,1)} %param.12) | copy-start | bytes 3145732
  399.8 782.4 %reduce-scatter.23.cloned.1.call-start = ((), (), s32[]{:S(2)}) async-start(), calls=%async_computation.28 | async-start | bytes 1310720 | tf_op jit(solution)/shard_map/reduce_scatter | solution.py:84
  435.5 620.0 %copy-start.14 = (f32[256,64]{0,1:T(8,128)}, f32[256,64]{0,1:T(8,128)S(1)}, u32[]{:S(2)}) copy-start(f32[256,64]{0,1:T(8,128)S(1)} %fusion.47) | copy-start | bytes 196612
  440.3 64.6 %copy-start.19 = (bf16[256,256]{0,1:T(8,128)(2,1)}, bf16[256,256]{0,1:T(8,128)(2,1)S(1)}, u32[]{:S(2)}) copy-start(bf16[256,256]{0,1:T(8,128)(2,1)S(1)} %convolution_convert_fusion.8) | copy-start | bytes 393220
  501.8 1.4 copy-start.5
  503.2 4.5 copy-start
  560.4 459.0 %copy-start.3 = (f32[256,2048]{1,0:T(8,128)}, f32[256,2048]{1,0:T(8,128)S(1)}, u32[]{:S(2)}) copy-start(f32[256,2048]{1,0:T(8,128)S(1)} %get-tuple-element.35) | copy-start | bytes 6291460
  1045.1 5.7 slice-start
  1045.1 6.2 slice-start.1
  1051.3 2.0 copy-start.6
  1053.3 2.1 copy-start.1
  1053.3 2.1 copy-start.18
  1057.7 125.0 %reduce-scatter.27.cloned.1.call-start = ((), (), s32[]{:S(2)}) async-start(), calls=%async_computation.30 | async-start | bytes 1310720 | tf_op jit(solution)/shard_map/reduce_scatter | solution.py:87
  1064.5 120.5 %reduce-scatter.19.cloned.1.call-start = ((), (), s32[]{:S(2)}) async-start(), calls=%async_computation.26 | async-start | bytes 10485760 | tf_op jit(solution)/shard_map/reduce_scatter | solution.py:81
  1076.1 183.3 %reduce-scatter.31.cloned.1.call-start = ((), (), s32[]{:S(2)}) async-start(), calls=%async_computation.32 | async-start | bytes 10485760 | tf_op jit(solution)/shard_map/reduce_scatter | solution.py:90
  1083.0 345.6 %reduce-scatter.43.cloned.1.call-start = ((), (), s32[]{:S(2)}) async-start(), calls=%async_computation.38 | async-start | bytes 28835840
  1127.0 471.0 %reduce-scatter.45.cloned.1.call-start = ((), (), s32[]{:S(2)}) async-start(), calls=%async_computation.39 | async-start | bytes 28835840
  1169.4 598.0 %reduce-scatter.39.cloned.1.call-start = ((), (), s32[]{:S(2)}) async-start(), calls=%async_computation.36 | async-start | bytes 28835840 | tf_op jit(solution)/shard_map/reduce_scatter | solution.py:127
  1182.1 650.5 %reduce-scatter.25.cloned.1.call-start = ((), (), s32[]{:S(2)}) async-start(), calls=%async_computation.29 | async-start | bytes 294912 | tf_op jit(solution)/shard_map/reduce_scatter | solution.py:101
  1182.7 714.4 %reduce-scatter.29.cloned.1.call-start = ((), (), s32[]{:S(2)}) async-start(), calls=%async_computation.31 | async-start | bytes 294912 | tf_op jit(solution)/shard_map/reduce_scatter | solution.py:104
  1183.4 784.3 %reduce-scatter.21.cloned.1.call-start = ((), (), s32[]{:S(2)}) async-start(), calls=%async_computation.27 | async-start | bytes 2359296 | tf_op jit(solution)/shard_map/reduce_scatter | solution.py:98
  1185.0 854.0 %reduce-scatter.33.cloned.1.call-start = ((), (), s32[]{:S(2)}) async-start(), calls=%async_computation.33 | async-start | bytes 2359296 | tf_op jit(solution)/shard_map/reduce_scatter | solution.py:107
  1259.4 892.5 %reduce-scatter.35.cloned.1.call-start = ((), (), s32[]{:S(2)}) async-start(), calls=%async_computation.34 | async-start | bytes 6488064 | tf_op jit(solution)/shard_map/reduce_scatter | solution.py:135
  1436.9 828.9 %reduce-scatter.37.cloned.1.call-start = ((), (), s32[]{:S(2)}) async-start(), calls=%async_computation.35 | async-start | bytes 6488064 | tf_op jit(solution)/shard_map/reduce_scatter | solution.py:138
  1606.5 773.5 %reduce-scatter.41.cloned.1.call-start = ((), (), s32[]{:S(2)}) async-start(), calls=%async_computation.37 | async-start | bytes 6488064 | tf_op jit(solution)/shard_map/reduce_scatter | solution.py:141
  1770.6 6.2 copy-start.12
  1770.6 6.2 copy-start.17
  1814.2 3.3 copy-start.4
  1814.2 3.3 copy-start.7
  (7 other events, 6.3 us)
Sparse Core Ops, SparseCore 0:
  10.7 55.1 all-gather.18
  68.6 49.7 all-gather.22
  121.1 90.8 all-gather.26
  214.6 90.8 all-gather.30
  307.9 91.7 all-gather.34
  401.1 14.9 all-gather.16
  417.7 16.7 all-gather.14
  436.0 58.2 all-gather.20
  495.9 58.2 all-gather.24
  555.6 143.1 all-gather.28
  700.4 143.1 all-gather.32
  844.9 143.2 all-gather.36
  1057.9 24.8 reduce-scatter.22
  1085.9 24.8 reduce-scatter.26
  1113.2 71.7 reduce-scatter.18
  1187.6 71.6 reduce-scatter.30
  1261.8 166.7 reduce-scatter.42
  1431.2 166.7 reduce-scatter.44
  1600.6 166.7 reduce-scatter.38
  1771.0 61.6 reduce-scatter.24
  1836.3 60.6 reduce-scatter.28
  1901.0 66.6 reduce-scatter.20
  1971.7 67.2 reduce-scatter.32
  2043.0 108.9 reduce-scatter.34
  2156.0 109.7 reduce-scatter.36
  2269.8 110.1 reduce-scatter.40
where the time goes:
time: 2400 us; the launch traced here: 2390 us
  waiting for transfers between devices  1920 us (80%)
  matrix products  189 us (8%)
  blocking collectives  135 us (6%)
  local copies, waits for them, and re-layouts  88.9 us (4%)
  other arithmetic  35.7 us (1%)
    unnamed x28, waiting for transfers between devices  333 us
    reduce_scatter x1, waiting for transfers between devices, reduce_feed(): lax.psum_scatter(grad_down.astype(jnp.bfloat16), 'fsdp', scatter_dimensio...  161 us
    all_gather x1, waiting for transfers between devices, feed_weights(): lax.all_gather(rows_full[1], 'fsdp', axis=1, tiled=True)  137 us
    all_gather x1, waiting for transfers between devices, feed_weights(): lax.all_gather(rows_full[2], 'fsdp', axis=1, tiled=True)  132 us
    all_gather x1, waiting for transfers between devices, feed_weights(): lax.all_gather(rows_full[3], 'fsdp', axis=0, tiled=True)  132 us
    reduce_scatter x1, waiting for transfers between devices, reduce_feed(): lax.psum_scatter(terms[3].astype(jnp.bfloat16), 'dp', scatter_dimension=1...  112 us
    reduce_scatter x1, waiting for transfers between devices, reduce_feed(): lax.psum_scatter(terms[2].astype(jnp.bfloat16), 'dp', scatter_dimension=0...  112 us
    reduce_scatter x1, waiting for transfers between devices, reduce_feed(): lax.psum_scatter(terms[1].astype(jnp.bfloat16), 'dp', scatter_dimension=0...  111 us
  transfers between devices with their start and end apart: 26, of which 21 were waited for; matrix products, arithmetic and copies ran while one was open for 10% of the time, Pallas kernels for 0%

commit v1 on v0

--- a/solution.py
+++ b/solution.py
@@ -7,6 +7,30 @@
 HEAD_DIM = 64
 EPSILON = 1e-05
 rope_base = 10000.0
+
+
+def render_sample_now(block_in, ndim_at):
+    local_out = list(block_in.shape[1:])
+    local_out[ndim_at] *= block_in.shape[0]
+    return jnp.moveaxis(block_in, 0, ndim_at).reshape(local_out)
+
+
+def _fit_sums_all(load, shard_axis):
+    parts_n = lax.psum(1, shard_axis)
+    value_now = load[None]
+    for idx in range(parts_n.bit_length() - 1):
+        next_value = 1 << idx
+        row_out = tuple(((j, j ^ next_value) for j in range(parts_n)))
+        w_next = lax.ppermute(value_now, shard_axis, row_out)
+        work_now = jnp.stack([value_now, w_next])
+        wide_out = lax.axis_index(shard_axis) >> idx & 1
+        value_now = jnp.where(wide_out == 0, work_now, work_now[::-1]).reshape(-1, *load.shape)
+    return value_now
+
+
+def solve_words(unit, sample, array_dim):
+    all_values = _fit_sums_all(unit, sample)
+    return render_sample_now(all_values, array_dim)
 
 
 def tables(segment_block):
@@ -60,7 +84,7 @@
         lax.all_gather(gain_mlp.astype(low_type), "dp", axis=0, tiled=True),
         lax.all_gather(w_gate.astype(low_type), "dp", axis=0, tiled=True),
         lax.all_gather(w_up.astype(low_type), "dp", axis=0, tiled=True),
-        lax.all_gather(w_down.astype(low_type), "dp", axis=1, tiled=True),
+        solve_words(w_down.astype(low_type), "dp", 1),
     )
     wide_cols = (
         lax.all_gather(rows_full[1], "fsdp", axis=1, tiled=True),

time: 2400 us -> 2300 us (0.958)
  waiting for transfers between devices: 1920 us -> 1810 us
    ppermute x0 -> x3, waiting for transfers between devices: none -> 168 us  [_fit_sums_all(): w_next = lax.ppermute(value_now, shard_axis, row_out)]
    all_gather x1 -> x0, waiting for transfers between devices: 94.2 us -> none  [feed_weights(): lax.all_gather(w_down.astype(low_type), 'dp', axis=1, tiled=True)]
    all_gather x1, waiting for transfers between devices: 137 us -> 46.2 us  [feed_weights(): lax.all_gather(rows_full[1], 'fsdp', axis=1, tiled=True)]
    all_gather x1, waiting for transfers between devices: 54 us -> 0.02 us  [attention_weights(): lax.all_gather(rows_full[1], 'fsdp', axis=1, tiled=True)]
    all_gather x1, waiting for transfers between devices: 43.9 us -> 0.01 us  [attention_weights(): lax.all_gather(rows_full[4], 'fsdp', axis=0, tiled=True)]
    unnamed x72 -> x68, local copies, waits for them, and re-layouts: 86.6 us -> 86.2 us
    unnamed x28 -> x27, waiting for transfers between devices: 333 us -> 333 us
  transfers between devices with their start and end apart: 26 -> 28, of which waited for: 21 -> 21; matrix products, arithmetic and copies ran while one was open for 10% -> 11% of each run, Pallas kernels for 0% -> 0%
where the time goes in v1:
time: 2300 us; the launch traced here: 2290 us
  waiting for transfers between devices  1810 us (79%)
  matrix products  188 us (8%)
  blocking collectives  138 us (6%)
  local copies, waits for them, and re-layouts  94 us (4%)
  other arithmetic  44.2 us (2%)
    unnamed x27, waiting for transfers between devices  333 us
    ppermute x3, waiting for transfers between devices, _fit_sums_all(): w_next = lax.ppermute(value_now, shard_axis, row_out)  168 us
    reduce_scatter x1, waiting for transfers between devices, reduce_feed(): lax.psum_scatter(grad_down.astype(jnp.bfloat16), 'fsdp', scatter_dimensio...  161 us
    all_gather x1, waiting for transfers between devices, feed_weights(): lax.all_gather(rows_full[3], 'fsdp', axis=0, tiled=True)  132 us
    all_gather x1, waiting for transfers between devices, feed_weights(): lax.all_gather(rows_full[2], 'fsdp', axis=1, tiled=True)  131 us
    reduce_scatter x1, waiting for transfers between devices, reduce_feed(): lax.psum_scatter(terms[3].astype(jnp.bfloat16), 'dp', scatter_dimension=1...  112 us
    reduce_scatter x1, waiting for transfers between devices, reduce_feed(): lax.psum_scatter(terms[2].astype(jnp.bfloat16), 'dp', scatter_dimension=0...  111 us
    reduce_scatter x1, waiting for transfers between devices, reduce_feed(): lax.psum_scatter(terms[1].astype(jnp.bfloat16), 'dp', scatter_dimension=0...  111 us
  transfers between devices with their start and end apart: 28, of which 21 were waited for; matrix products, arithmetic and copies ran while one was open for 11% of the time, Pallas kernels for 0%

profile of v1, /device:TPU:0, one launch (start us, length us, event | category | flops | bytes accessed | tf_op | source)
XLA Modules:
  0.0 2292.9 jit_solution(6098093577211236838)
XLA Ops:
  13.2 35.4 %all_gather.61 = bf16[2048,64]{0,1:T(8,128)(2,1)} all-gather(bf16[256,64]{0,1:T(8,128)(2,1)S(1)} %convert_element_type.225), channel_id=1, replica_groups=mesh['dp'=8,'fsdp'=4] {'dp'}, dimensions={0}, use_global_device_ids=true | all-gather | bytes 294912 | tf_op jit(solution)/shard_map/all_gather | solution.py:68
  48.7 33.3 %all_gather.59 = bf16[2048,64]{0,1:T(8,128)(2,1)} all-gather(bf16[256,64]{0,1:T(8,128)(2,1)S(1)} %convert_element_type.223), channel_id=1, replica_groups=mesh['dp'=8,'fsdp'=4] {'dp'}, dimensions={0}, use_global_device_ids=true | all-gather | bytes 294912 | tf_op jit(solution)/shard_map/all_gather | solution.py:69
  82.8 35.5 %all-gather.22.cloned.1.call-done = bf16[512,2048]{1,0:T(8,128)(2,1)} async-done(((bf16[512,256]{1,0:T(8,128)(2,1)}), bf16[512,2048]{1,0:T(8,128)(2,1)}) %all-gather.22.cloned.1.call-update) | async-done | bytes 2097168 | tf_op jit(solution)/shard_map/all_gather | solution.py:70
  118.4 93.6 %all-gather.26.cloned.1.call-done = bf16[2048,1408]{1,0:T(8,128)(2,1)} async-done(((bf16[256,1408]{1,0:T(8,128)(2,1)}), bf16[2048,1408]{1,0:T(8,128)(2,1)}) %all-gather.26.cloned.1.call-update) | async-done | bytes 5767184 | tf_op jit(solution)/shard_map/all_gather | solution.py:85
  212.0 93.4 %all-gather.30.cloned.1.call-done = bf16[2048,1408]{1,0:T(8,128)(2,1)} async-done(((bf16[256,1408]{1,0:T(8,128)(2,1)}), bf16[2048,1408]{1,0:T(8,128)(2,1)}) %all-gather.30.cloned.1.call-update) | async-done | bytes 5767184 | tf_op jit(solution)/shard_map/all_gather | solution.py:86
  307.5 16.6 collective-permute-done
  324.7 31.8 %collective-permute-done.1 = bf16[2,1408,256]{2,1,0:T(8,128)(2,1)} collective-permute-done((bf16[2,1408,256]{2,1,0:T(8,128)(2,1)S(1)}, bf16[2,1408,256]{2,1,0:T(8,128)(2,1)}, u32[]{:S(2)}, u32[]{:S(2)}) %collective-permute-start.1) | collective-permute-done | bytes 1441824 | tf_op jit(solution)/shard_map/ppermute | solution.py:24
  366.3 120.0 %collective-permute-done.2 = bf16[4,1408,256]{1,2,0:T(8,128)(2,1)} collective-permute-done((bf16[4,1408,256]{1,2,0:T(8,128)(2,1)}, bf16[4,1408,256]{1,2,0:T(8,128)(2,1)}, u32[]{:S(2)}, u32[]{:S(2)}) %collective-permute-start.2) | collective-permute-done | bytes 2883616 | tf_op jit(solution)/shard_map/ppermute | solution.py:24
  486.3 3.3 pad_maximum_fusion
  489.6 3.6 reverse_select_fusion
  493.9 19.7 all-gather
  513.6 16.6 all-gather.1
  535.5 6.9 fusion.53
  550.4 6.2 multiply_reduce_fusion.2
  558.3 46.2 %all-gather.28.cloned.1.call-done = bf16[2048,5632]{1,0:T(8,128)(2,1)} async-done(((bf16[2048,1408]{1,0:T(8,128)(2,1)}), bf16[2048,5632]{1,0:T(8,128)(2,1)}) %all-gather.28.cloned.1.call-update) | async-done | bytes 23068688 | tf_op jit(solution)/shard_map/all_gather | solution.py:90
  604.5 13.1 fusion.59
  617.6 131.4 %all-gather.32.cloned.1.call-done = bf16[2048,5632]{1,0:T(8,128)(2,1)} async-done(((bf16[2048,1408]{1,0:T(8,128)(2,1)}), bf16[2048,5632]{1,0:T(8,128)(2,1)}) %all-gather.32.cloned.1.call-update) | async-done | bytes 23068688 | tf_op jit(solution)/shard_map/all_gather | solution.py:91
  749.0 13.0 fusion.60
  762.1 131.7 %all-gather.34.cloned.1.call-done = bf16[5632,2048]{0,1:T(8,128)(2,1)} async-done(((bf16[1408,2048]{0,1:T(8,128)(2,1)}), bf16[5632,2048]{0,1:T(8,128)(2,1)}) %all-gather.34.cloned.1.call-update) | async-done | bytes 23068688 | tf_op jit(solution)/shard_map/all_gather | solution.py:92
  893.8 17.1 multiply_convert_fusion
  910.8 12.6 fusion.61
  923.4 13.4 multiply_reduce_fusion
  940.0 6.7 convolution_convert_fusion.7
  949.0 5.6 fusion
  961.6 5.1 fusion.35
  974.1 5.8 convolution_convert_fusion.4
  980.0 6.8 convolution_convert_fusion.3
  986.9 13.0 convolution_convert_fusion.2
  999.9 30.8 %copy.73 = bf16[2048,5632]{0,1:T(8,128)(2,1)} copy(bf16[2048,5632]{1,0:T(8,128)(2,1)} %convolution_convert_fusion.2) | data formatting | bytes 46137344
  1031.2 13.2 convolution_convert_fusion.1
  1044.4 28.9 %copy.75 = bf16[2048,5632]{0,1:T(8,128)(2,1)} copy(bf16[2048,5632]{1,0:T(8,128)(2,1)} %convolution_convert_fusion.1) | data formatting | bytes 46137344
  1073.4 12.6 convolution_convert_fusion
  1089.0 74.3 %reduce-scatter.31.cloned.1.call-done = bf16[512,2048]{1,0:T(8,128)(2,1)} async-done(((bf16[2048,2048]{1,0:T(8,128)(2,1)}), bf16[512,2048]{1,0:T(8,128)(2,1)}) %reduce-scatter.31.cloned.1.call-update) | async-done | bytes 2097168 | tf_op jit(solution)/shard_map/reduce_scatter | solution.py:114
  1163.4 169.2 %reduce-scatter.43.cloned.1.call-done = bf16[1408,2048]{1,0:T(8,128)(2,1)} async-done(((bf16[5632,2048]{1,0:T(8,128)(2,1)}), bf16[1408,2048]{1,0:T(8,128)(2,1)}) %reduce-scatter.43.cloned.1.call-update) | async-done | bytes 5767184
  1332.6 8.2 copy.74
  1340.9 161.1 %reduce-scatter.45.cloned.1.call-done = bf16[1408,2048]{1,0:T(8,128)(2,1)} async-done(((bf16[5632,2048]{1,0:T(8,128)(2,1)}), bf16[1408,2048]{1,0:T(8,128)(2,1)}) %reduce-scatter.45.cloned.1.call-update) | async-done | bytes 5767184
  1502.0 8.4 copy.76
  1510.4 160.8 %reduce-scatter.39.cloned.1.call-done = bf16[1408,2048]{1,0:T(8,128)(2,1)} async-done(((bf16[5632,2048]{1,0:T(8,128)(2,1)}), bf16[1408,2048]{1,0:T(8,128)(2,1)}) %reduce-scatter.39.cloned.1.call-update) | async-done | bytes 5767184 | tf_op jit(solution)/shard_map/reduce_scatter | solution.py:151
  1674.4 6.2 fusion.62
  1684.1 10.7 all-reduce.5
  1694.8 21.8 all-reduce.4
  1721.1 12.9 fusion.16
  1738.0 62.9 %reduce-scatter.29.cloned.1.call-done = bf16[256,64]{0,1:T(8,128)(2,1)} async-done(((bf16[2048,64]{0,1:T(8,128)(2,1)}), bf16[256,64]{0,1:T(8,128)(2,1)}) %reduce-scatter.29.cloned.1.call-update) | async-done | bytes 32784 | tf_op jit(solution)/shard_map/reduce_scatter | solution.py:128
  1802.3 69.2 %reduce-scatter.21.cloned.1.call-done = bf16[256,512]{1,0:T(8,128)(2,1)} async-done(((bf16[2048,512]{1,0:T(8,128)(2,1)}), bf16[256,512]{1,0:T(8,128)(2,1)}) %reduce-scatter.21.cloned.1.call-update) | async-done | bytes 262160 | tf_op jit(solution)/shard_map/reduce_scatter | solution.py:122
  1873.3 69.3 %reduce-scatter.33.cloned.1.call-done = bf16[512,256]{1,0:T(8,128)(2,1)} async-done(((bf16[512,2048]{1,0:T(8,128)(2,1)}), bf16[512,256]{1,0:T(8,128)(2,1)}) %reduce-scatter.33.cloned.1.call-update) | async-done | bytes 262160 | tf_op jit(solution)/shard_map/reduce_scatter | solution.py:131
  1944.4 111.3 %reduce-scatter.35.cloned.1.call-done = bf16[256,1408]{1,0:T(8,128)(2,1)} async-done(((bf16[2048,1408]{1,0:T(8,128)(2,1)}), bf16[256,1408]{1,0:T(8,128)(2,1)}) %reduce-scatter.35.cloned.1.call-update) | async-done | bytes 720912 | tf_op jit(solution)/shard_map/reduce_scatter | solution.py:159
  2058.1 111.5 %reduce-scatter.37.cloned.1.call-done = bf16[256,1408]{1,0:T(8,128)(2,1)} async-done(((bf16[2048,1408]{1,0:T(8,128)(2,1)}), bf16[256,1408]{1,0:T(8,128)(2,1)}) %reduce-scatter.37.cloned.1.call-update) | async-done | bytes 720912 | tf_op jit(solution)/shard_map/reduce_scatter | solution.py:162
  2171.8 112.0 %reduce-scatter.41.cloned.1.call-done = bf16[1408,256]{1,0:T(8,128)(2,1)} async-done(((bf16[1408,2048]{1,0:T(8,128)(2,1)}), bf16[1408,256]{1,0:T(8,128)(2,1)}) %reduce-scatter.41.cloned.1.call-update) | async-done | bytes 720912 | tf_op jit(solution)/shard_map/reduce_scatter | solution.py:165
  (192 shorter events, 83.7 us)
Async XLA Ops:
  7.2 3.9 copy-start.7
  7.2 5.0 copy-start.8
  7.2 74.9 %all-gather.18.cloned.1.call-start = ((), (), s32[]{:S(2)}) async-start(), calls=%async_computation.16 | async-start | bytes 2359296 | tf_op jit(solution)/shard_map/all_gather | solution.py:67
  9.2 109.1 %all-gather.22.cloned.1.call-start = ((), (), s32[]{:S(2)}) async-start(), calls=%async_computation.18 | async-start | bytes 2359296 | tf_op jit(solution)/shard_map/all_gather | solution.py:70
  11.0 2.1 copy-start.18
  11.1 37.6 %copy-start.19 = (f32[256,64]{0,1:T(8,128)S(1)}, f32[256,64]{0,1:T(8,128)}, u32[]{:S(2)}) copy-start(f32[256,64]{0,1:T(8,128)} %param.17) | copy-start | bytes 196612
  11.1 200.9 %all-gather.26.cloned.1.call-start = ((), (), s32[]{:S(2)}) async-start(), calls=%async_computation.20 | async-start | bytes 6488064 | tf_op jit(solution)/shard_map/all_gather | solution.py:85
  12.1 293.3 %all-gather.30.cloned.1.call-start = ((), (), s32[]{:S(2)}) async-start(), calls=%async_computation.22 | async-start | bytes 6488064 | tf_op jit(solution)/shard_map/all_gather | solution.py:86
  13.1 518.6 %all-gather.16.cloned.1.call-start = ((), (), s32[]{:S(2)}) async-start(), calls=%async_computation.15 | async-start | bytes 1310720 | tf_op jit(solution)/shard_map/all_gather | solution.py:74
  48.6 485.1 %all-gather.14.cloned.1.call-start = ((), (), s32[]{:S(2)}) async-start(), calls=%async_computation.14 | async-start | bytes 1310720 | tf_op jit(solution)/shard_map/all_gather | solution.py:75
  82.0 453.5 %all-gather.20.cloned.1.call-start = ((), (), s32[]{:S(2)}) async-start(), calls=%async_computation.17 | async-start | bytes 10485760 | tf_op jit(solution)/shard_map/all_gather | solution.py:73
  82.8 467.6 %all-gather.24.cloned.1.call-start = ((), (), s32[]{:S(2)}) async-start(), calls=%async_computation.19 | async-start | bytes 10485760 | tf_op jit(solution)/shard_map/all_gather | solution.py:76
  118.4 486.1 %all-gather.28.cloned.1.call-start = ((), (), s32[]{:S(2)}) async-start(), calls=%async_computation.21 | async-start | bytes 28835840 | tf_op jit(solution)/shard_map/all_gather | solution.py:90
  212.0 537.0 %all-gather.32.cloned.1.call-start = ((), (), s32[]{:S(2)}) async-start(), calls=%async_computation.23 | async-start | bytes 28835840 | tf_op jit(solution)/shard_map/all_gather | solution.py:91
  305.4 1.4 copy-start.9
  305.5 588.3 %all-gather.34.cloned.1.call-start = ((), (), s32[]{:S(2)}) async-start(), calls=%async_computation.24 | async-start | bytes 28835840 | tf_op jit(solution)/shard_map/all_gather | solution.py:92
  306.9 17.3 collective-permute-start
  324.6 31.9 %collective-permute-start.1 = (bf16[2,1408,256]{2,1,0:T(8,128)(2,1)S(1)}, bf16[2,1408,256]{2,1,0:T(8,128)(2,1)}, u32[]{:S(2)}, u32[]{:S(2)}) collective-permute-start(bf16[2,1408,256]{2,1,0:T(8,128)(2,1)S(1)} %get-tuple-element.27), channel_id=1, source_target_pairs={{0,8},{4,12},{8,0},{12,4},{16,24},{20,28},{24,16},{28,20},{1,9},{5... | collective-permute-start | bytes 4325384 | tf_op jit(solution)/shard_map/ppermute | solution.py:24
  361.5 124.8 %collective-permute-start.2 = (bf16[4,1408,256]{1,2,0:T(8,128)(2,1)}, bf16[4,1408,256]{1,2,0:T(8,128)(2,1)}, u32[]{:S(2)}, u32[]{:S(2)}) collective-permute-start(bf16[4,1408,256]{1,2,0:T(8,128)(2,1)} %copy.56), channel_id=1, source_target_pairs={{0,16},{4,20},{8,24},{12,28},{16,0},{20,4},{24,8},{28,12},{1,17},{... | collective-permute-start | bytes 8650760 | tf_op jit(solution)/shard_map/ppermute | solution.py:24
  493.2 20.4 copy-start.22
  493.2 37.0 %copy-start.20 = (s32[256]{0:T(256)S(1)}, s32[256]{0:T(256)}, u32[]{:S(2)}) copy-start(s32[256]{0:T(256)} %param.13) | copy-start | bytes 3076
  493.2 38.1 %copy-start.2 = (bf16[256,2048]{1,0:T(8,128)(2,1)S(1)}, bf16[256,2048]{1,0:T(8,128)(2,1)}, u32[]{:S(2)}) copy-start(bf16[256,2048]{1,0:T(8,128)(2,1)} %param.12) | copy-start | bytes 3145732
  493.2 592.9 %reduce-scatter.23.cloned.1.call-start = ((), (), s32[]{:S(2)}) async-start(), calls=%async_computation.27 | async-start | bytes 1310720 | tf_op jit(solution)/shard_map/reduce_scatter | solution.py:108
  530.6 428.6 %copy-start.12 = (f32[256,64]{0,1:T(8,128)}, f32[256,64]{0,1:T(8,128)S(1)}, u32[]{:S(2)}) copy-start(f32[256,64]{0,1:T(8,128)S(1)} %fusion.49) | copy-start | bytes 196612
  535.5 10.6 copy-start.17
  543.0 1.4 copy-start.4
  544.4 3.4 copy-start
  556.5 366.9 %copy-start.3 = (f32[256,2048]{1,0:T(8,128)}, f32[256,2048]{1,0:T(8,128)S(1)}, u32[]{:S(2)}) copy-start(f32[256,2048]{1,0:T(8,128)S(1)} %get-tuple-element.39) | copy-start | bytes 6291460
  949.0 5.7 slice-start
  949.0 6.2 slice-start.1
  955.2 2.0 copy-start.5
  957.2 2.1 copy-start.1
  957.2 2.1 copy-start.16
  961.6 125.3 %reduce-scatter.27.cloned.1.call-start = ((), (), s32[]{:S(2)}) async-start(), calls=%async_computation.29 | async-start | bytes 1310720 | tf_op jit(solution)/shard_map/reduce_scatter | solution.py:111
  968.3 120.7 %reduce-scatter.19.cloned.1.call-start = ((), (), s32[]{:S(2)}) async-start(), calls=%async_computation.25 | async-start | bytes 10485760 | tf_op jit(solution)/shard_map/reduce_scatter | solution.py:105
  980.0 183.4 %reduce-scatter.31.cloned.1.call-start = ((), (), s32[]{:S(2)}) async-start(), calls=%async_computation.31 | async-start | bytes 10485760 | tf_op jit(solution)/shard_map/reduce_scatter | solution.py:114
  986.9 345.7 %reduce-scatter.43.cloned.1.call-start = ((), (), s32[]{:S(2)}) async-start(), calls=%async_computation.37 | async-start | bytes 28835840
  1030.8 471.2 %reduce-scatter.45.cloned.1.call-start = ((), (), s32[]{:S(2)}) async-start(), calls=%async_computation.38 | async-start | bytes 28835840
  1073.4 597.9 %reduce-scatter.39.cloned.1.call-start = ((), (), s32[]{:S(2)}) async-start(), calls=%async_computation.35 | async-start | bytes 28835840 | tf_op jit(solution)/shard_map/reduce_scatter | solution.py:151
  1086.1 650.6 %reduce-scatter.25.cloned.1.call-start = ((), (), s32[]{:S(2)}) async-start(), calls=%async_computation.28 | async-start | bytes 294912 | tf_op jit(solution)/shard_map/reduce_scatter | solution.py:125
  1086.8 714.1 %reduce-scatter.29.cloned.1.call-start = ((), (), s32[]{:S(2)}) async-start(), calls=%async_computation.30 | async-start | bytes 294912 | tf_op jit(solution)/shard_map/reduce_scatter | solution.py:128
  1087.4 784.1 %reduce-scatter.21.cloned.1.call-start = ((), (), s32[]{:S(2)}) async-start(), calls=%async_computation.26 | async-start | bytes 2359296 | tf_op jit(solution)/shard_map/reduce_scatter | solution.py:122
  1089.0 853.7 %reduce-scatter.33.cloned.1.call-start = ((), (), s32[]{:S(2)}) async-start(), calls=%async_computation.32 | async-start | bytes 2359296 | tf_op jit(solution)/shard_map/reduce_scatter | solution.py:131
  1163.3 892.4 %reduce-scatter.35.cloned.1.call-start = ((), (), s32[]{:S(2)}) async-start(), calls=%async_computation.33 | async-start | bytes 6488064 | tf_op jit(solution)/shard_map/reduce_scatter | solution.py:159
  1340.8 828.7 %reduce-scatter.37.cloned.1.call-start = ((), (), s32[]{:S(2)}) async-start(), calls=%async_computation.34 | async-start | bytes 6488064 | tf_op jit(solution)/shard_map/reduce_scatter | solution.py:162
  1510.4 773.4 %reduce-scatter.41.cloned.1.call-start = ((), (), s32[]{:S(2)}) async-start(), calls=%async_computation.36 | async-start | bytes 6488064 | tf_op jit(solution)/shard_map/reduce_scatter | solution.py:165
  1674.4 6.2 copy-start.10
  1674.4 6.2 copy-start.15
  (7 other events, 6.3 us)
Sparse Core Ops, SparseCore 0:
  10.7 54.9 all-gather.17
  68.3 49.9 all-gather.21
  121.1 90.8 all-gather.25
  214.6 90.8 all-gather.29
  306.8 14.9 all-gather.15
  323.2 16.7 all-gather.13
  341.5 58.2 all-gather.19
  401.4 58.2 all-gather.23
  461.3 143.1 all-gather.27
  605.9 143.1 all-gather.31
  750.6 143.1 all-gather.33
  961.7 24.8 reduce-scatter.22
  989.9 24.8 reduce-scatter.26
  1017.2 71.7 reduce-scatter.18
  1091.6 71.6 reduce-scatter.30
  1165.8 166.7 reduce-scatter.42
  1335.2 166.7 reduce-scatter.44
  1504.4 166.7 reduce-scatter.38
  1674.9 61.6 reduce-scatter.24
  1740.2 60.6 reduce-scatter.28
  1804.8 66.6 reduce-scatter.20
  1875.5 67.1 reduce-scatter.32
  1946.8 108.9 reduce-scatter.34
  2059.7 109.7 reduce-scatter.36
  2173.6 110.1 reduce-scatter.40
